TPU v7x, 32 devices: a whole 2x2x4 slice. The times are simulated.
32 devices in a mesh: row: 16 (over z, y, x), col: 2 (over core).
Axes of the slice: x: 2, y: 2, z: 4, core: 2. Of those that a mesh axis runs over, the one named last changes fastest.
Arguments:
- matrix: float32 [4096, 4096], P('row', 'col'), may hold values from -15.625 to 15.625
Outputs:
- r_top: float32 [512, 4096], P(None, 'col')
- basis: float32 [4096, 512], P('row')
All inputs are finite; a program needn't handle non-finite values.
Results may differ from a plain program's by a relative error of at most 0.0003.
Values sent between devices are 32-bit elements; how exact they have to be, the bound alone decides.
A program may use at most 64 MiB of HBM per device.

v0:
```python
import functools
import math

import jax
import jax.numpy as jnp
from jax import lax
from jax.experimental import pallas as pl
from jax.experimental.pallas import tpu as pltpu
from jax.sharding import PartitionSpec as P

PANEL = 256
WIDE = 2 * PANEL
LANE = 128
SUB = 8
HIGHEST = lax.Precision.HIGHEST
MESH = pl.DeviceIdType.MESH


def dot(a, b, ca=1, cb=0):
    return lax.dot_general(
        a, b, (((ca,), (cb,)), ((), ())), precision=HIGHEST, preferred_element_type=jnp.float32
    )


def row_chunks(rows):
    units = rows // SUB
    sizes = [units // 3 + (1 if i < units % 3 else 0) for i in range(3)]
    out, at = [], 0
    for size in sizes:
        if size:
            out.append((at * SUB, size * SUB))
            at += size
    return out


class AllReduce:
    def __init__(self, src, recv, dst, sems, n_row, me, col):
        self.src, self.recv, self.dst = src, recv, dst
        self.sems = sems
        self.n = n_row
        self.bits = n_row.bit_length() - 1
        self.col = col
        self.me = me
        self.chunks = []
        spin = max(self.bits - 1, 1)
        for c, (ro, rn) in enumerate(row_chunks(src.shape[1])):
            order = [(c + t) % spin for t in range(spin)] + list(range(spin, self.bits))
            starts = [0]
            mine = []
            for s, b in enumerate(order):
                bit = (me // (1 << b)) % 2
                mine.append(bit)
                starts.append(starts[-1] + bit * (n_row >> (s + 1)))
            self.chunks.append((c, ro, rn, order, starts, mine))

    def partner(self, b, bit):
        return self.me + (1 << b) * (1 - 2 * bit)

    def rs_copy(self, s, chunk):
        c, ro, rn, order, starts, mine = chunk
        half = self.n >> (s + 1)
        off = self.n - (self.n >> s)
        bit = mine[s]
        send = starts[s] + (1 - bit) * half
        return pltpu.make_async_remote_copy(
            src_ref=self.src.at[pl.ds(send, half), pl.ds(ro, rn), :],
            dst_ref=self.recv.at[pl.ds(off, half), pl.ds(ro, rn), :],
            send_sem=self.sems.at[0, s, c],
            recv_sem=self.sems.at[1, s, c],
            device_id=(self.partner(order[s], bit), self.col),
            device_id_type=MESH,
        )

    def rs_start(self, s):
        for chunk in self.chunks:
            self.rs_copy(s, chunk).start()

    def rs_finish(self, s):
        half = self.n >> (s + 1)
        off = self.n - (self.n >> s)
        last = s == self.bits - 1
        for chunk in self.chunks:
            c, ro, rn, order, starts, mine = chunk
            self.rs_copy(s, chunk).wait()
            keep = starts[s + 1]
            into = self.dst if last else self.src

            def add(i, carry, ro=ro, rn=rn, keep=keep, into=into):
                rows = pl.ds(ro, rn)
                into[keep + i, rows, :] = self.src[keep + i, rows, :] + self.recv[off + i, rows, :]
                return carry

            lax.fori_loop(0, half, add, 0)
            if not last:
                self.rs_copy(s + 1, chunk).start()
            else:
                self.ag_copy(s, chunk).start()

    def ag_copy(self, s, chunk):
        c, ro, rn, order, starts, mine = chunk
        half = self.n >> (s + 1)
        bit = mine[s]
        region = self.dst.at[pl.ds(starts[s + 1], half), pl.ds(ro, rn), :]
        return pltpu.make_async_remote_copy(
            src_ref=region,
            dst_ref=region,
            send_sem=self.sems.at[2, s, c],
            recv_sem=self.sems.at[3, s, c],
            device_id=(self.partner(order[s], bit), self.col),
            device_id_type=MESH,
        )

    def ag_finish(self, s):
        for chunk in self.chunks:
            self.ag_copy(s, chunk).wait()
            if s > 0:
                self.ag_copy(s - 1, chunk).start()

    def steps(self):
        out = [functools.partial(self.rs_finish, s) for s in range(self.bits)]
        out += [functools.partial(self.ag_finish, s) for s in reversed(range(self.bits))]
        return out


def factor_panels(t_ref, k, lo, hi):
    base = k * LANE
    size = t_ref.shape[0]
    lane = lax.broadcasted_iota(jnp.int32, (SUB, LANE), 1)
    sub = lax.broadcasted_iota(jnp.int32, (SUB, LANE), 0)
    wide_lane = lax.broadcasted_iota(jnp.int32, (SUB, size), 1)
    wide_sub = lax.broadcasted_iota(jnp.int32, (SUB, size), 0)

    def one(p, carry):
        r0 = pl.multiple_of(base + p * SUB, SUB)
        pan = t_ref[pl.ds(r0, SUB), :]
        x = pltpu.roll(pan[:, base : base + LANE], (LANE - p * SUB) % LANE, 1)
        for j in range(SUB - 1):
            col = x[:, j : j + 1]
            m = jnp.where(sub[:, :1] > j, col / col[j : j + 1, :], 0.0)
            row = jnp.where(lane[:1] == j, 1.0, x[j : j + 1, :])
            x = jnp.where((lane == j) & (sub > j), 0.0, x) - m * row
        diag = jnp.sum(jnp.where(lane == sub, x, 0.0), axis=1, keepdims=True)
        scale = 1.0 / jnp.sqrt(diag)
        inv = jnp.where(lane == sub, 1.0, jnp.where(lane < sub, x, 0.0)) * scale
        rel = wide_lane - r0
        inside = (rel >= 0) & (rel < SUB)
        pan = jnp.where(inside, jnp.where(rel == wide_sub, 1.0, 0.0), pan)
        top = inv[:, 0:1] * pan[0:1, :]
        for j in range(1, SUB):
            top = top + inv[:, j : j + 1] * pan[j : j + 1, :]
        w = jnp.where(rel >= SUB, top, 0.0)
        upd = dot(w[:, base:], top, 0, 0)
        rel_all = lax.broadcasted_iota(jnp.int32, (size - base, size), 1) - r0
        clear = (rel_all >= 0) & (rel_all < SUB)
        t_ref[base:, :] = jnp.where(clear, 0.0, t_ref[base:, :]) - upd
        t_ref[pl.ds(r0, SUB), :] = top
        return carry

    lax.fori_loop(lo, hi, one, 0)


def kernel(n_row, n_col, scale, a_ref, top_ref, basis_ref, a12, a12t, p, p_in, q, g, g_in, gq, t,
           p_sems, g_sems, bsend, brecv):
    me = lax.axis_index("row")
    col = lax.axis_index("col")
    bits = n_row.bit_length() - 1
    blocks = a_ref.shape[1] // LANE
    gblocks = WIDE // LANE
    p_split = p.shape[0] // blocks
    g_split = g.shape[0] // gblocks

    barrier = pltpu.get_barrier_semaphore()
    for b in range(bits):
        bit = (me // (1 << b)) % 2
        pl.semaphore_signal(
            barrier, inc=1, device_id=(me + (1 << b) * (1 - 2 * bit), col), device_id_type=MESH
        )
    for c in range(1, n_col):
        pl.semaphore_signal(barrier, inc=1, device_id=(me, (col + c) % n_col), device_id_type=MESH)
    pl.semaphore_wait(barrier, bits + n_col - 1)

    def panel_copy(c):
        return pltpu.make_async_remote_copy(
            src_ref=a_ref.at[:, pl.ds(0, WIDE)],
            dst_ref=a12,
            send_sem=bsend.at[c],
            recv_sem=brecv.at[0],
            device_id=(me, c),
            device_id_type=MESH,
        )

    @pl.when(col == 0)
    def _():
        for c in range(1, n_col):
            panel_copy(c).start()
        a12[...] = a_ref[:, :WIDE]
        for c in range(1, n_col):
            panel_copy(c).wait_send()

    @pl.when(col != 0)
    def _():
        panel_copy(0).wait_recv()

    a12t[...] = a12[...].T

    def fill(dst, src, split):
        pair = 2 * LANE

        def one(i, carry):
            val = dot(a12t[...], src[:, pl.ds(pl.multiple_of(i * pair, pair), pair)])
            for h in range(2):
                part = val[:, h * LANE : (h + 1) * LANE]
                dst[pl.ds((2 * i + h) * split, split)] = part.reshape(split, WIDE // split, LANE)
            return carry

        lax.fori_loop(0, src.shape[1] // pair, one, 0)

    fill(g, a12, g_split)
    g_red = AllReduce(g, g_in, gq, g_sems, n_row, me, col)
    g_red.rs_start(0)
    fill(p, a_ref, p_split)
    for step in g_red.steps():
        step()
    p_red = AllReduce(p, p_in, q, p_sems, n_row, me, col)
    p_red.rs_start(0)
    for b in range(gblocks):
        t[:, b * LANE : (b + 1) * LANE] = gq[b * g_split : (b + 1) * g_split].reshape(WIDE, LANE)

    per = LANE // SUB
    units = [(k, lo, lo + per // 2) for k in range(gblocks) for lo in (0, per // 2)]
    steps = p_red.steps()
    done = 0
    for i, step in enumerate(steps):
        upto = len(units) * (i + 1) // len(steps)
        for unit in units[done:upto]:
            factor_panels(t, *unit)
        done = upto
        step()

    rows = lax.broadcasted_iota(jnp.int32, (WIDE, WIDE), 0)
    cols = lax.broadcasted_iota(jnp.int32, (WIDE, WIDE), 1)
    t[...] = jnp.where(cols <= rows, t[...], 0.0)
    basis_ref[...] = dot(a12[...], t[...], 1, 1) * scale

    def finish(i, carry):
        pair = 2 * LANE
        parts = [
            q[pl.ds((2 * i + h) * p_split, p_split)].reshape(WIDE, LANE) for h in range(2)
        ]
        val = dot(t[...], jnp.concatenate(parts, axis=1))
        r = lax.broadcasted_iota(jnp.int32, (WIDE, pair), 0)
        c = lax.broadcasted_iota(jnp.int32, (WIDE, pair), 1) + col * a_ref.shape[1] + i * pair
        top_ref[:, pl.ds(pl.multiple_of(i * pair, pair), pair)] = jnp.where(c >= r, val, 0.0)
        return carry

    lax.fori_loop(0, blocks // 2, finish, 0)


def body(n_row, n_col, matrix):
    height, width = matrix.shape
    scale = math.sqrt(height * n_row)
    bits = n_row.bit_length() - 1
    p_shape = (n_row, (width // LANE) * WIDE // n_row, LANE)
    g_shape = (n_row, (WIDE // LANE) * WIDE // n_row, LANE)
    f32 = jnp.float32
    vmem = pl.BlockSpec(memory_space=pltpu.VMEM)
    return pl.pallas_call(
        functools.partial(kernel, n_row, n_col, scale),
        out_shape=(
            jax.ShapeDtypeStruct((WIDE, width), f32),
            jax.ShapeDtypeStruct((height, WIDE), f32),
        ),
        in_specs=[vmem],
        out_specs=(vmem, vmem),
        scratch_shapes=[
            pltpu.VMEM((height, WIDE), f32),
            pltpu.VMEM((WIDE, height), f32),
            pltpu.VMEM(p_shape, f32),
            pltpu.VMEM(p_shape, f32),
            pltpu.VMEM(p_shape, f32),
            pltpu.VMEM(g_shape, f32),
            pltpu.VMEM(g_shape, f32),
            pltpu.VMEM(g_shape, f32),
            pltpu.VMEM((WIDE, WIDE), f32),
            pltpu.SemaphoreType.DMA((4, bits, 3)),
            pltpu.SemaphoreType.DMA((4, bits, 3)),
            pltpu.SemaphoreType.DMA((n_col,)),
            pltpu.SemaphoreType.DMA((1,)),
        ],
        compiler_params=pltpu.CompilerParams(
            collective_id=0, has_side_effects=True, vmem_limit_bytes=60 * 1024 * 1024
        ),
    )(matrix)


def solution(mesh):
    return jax.shard_map(
        functools.partial(body, mesh.shape["row"], mesh.shape["col"]),
        mesh=mesh,
        in_specs=(P("row", "col"),),
        out_specs=(P(None, "col"), P("row", None)),
        check_vma=False,
    )
```

profile of v0, /device:TPU:0, one launch (start us, length us, event | category | flops | bytes accessed | tf_op | source)
XLA Modules:
  0.0 164.1 jit_solution(12953860358832242898)
XLA Ops:
  0.6 157.9 %shard_map.30 = (f32[512,2048]{1,0:T(8,128)}, f32[256,512]{1,0:T(8,128)}) custom-call(f32[256,2048]{1,0:T(8,128)} %a_ref.1), custom_call_target="tpu_custom_call" | custom-call | tf_op jit(solution)/shard_map/pallas_call | solution.py:267
  158.5 0.0 copy-start
  158.5 4.8 %copy.5 = f32[512,2048]{1,0:T(8,128)} copy(f32[512,2048]{1,0:T(8,128)} %get-tuple-element.4) | data formatting | bytes 8388608
  163.3 0.0 copy-done
  163.3 0.8 copy.6
Async XLA Ops:
  158.5 4.8 %copy-start = (f32[256,512]{1,0:T(8,128)S(1)}, f32[256,512]{1,0:T(8,128)}, u32[]{:S(2)}) copy-start(f32[256,512]{1,0:T(8,128)} %get-tuple-element.5) | copy-start | bytes 1572868
where the time goes:
time: 164 us
  Pallas kernels  158 us (96%)
  local copies, waits for them, and re-layouts  5.55 us (3%)
    pallas_call x1, Pallas kernels, body(): pl.pallas_call(functools.partial(kernel, n_row, n_col, scale), out_shape=...  158 us
    unnamed x4, local copies, waits for them, and re-layouts  5.55 us

commit v1 on v0

--- a/solution.py
+++ b/solution.py
@@ -12,6 +12,7 @@
 WIDE = 2 * PANEL
 LANE = 128
 SUB = 8
+P_CHUNKS = 6
 HIGHEST = lax.Precision.HIGHEST
 MESH = pl.DeviceIdType.MESH
 
@@ -22,9 +23,9 @@
     )
 
 
-def row_chunks(rows):
+def row_chunks(rows, count):
     units = rows // SUB
-    sizes = [units // 3 + (1 if i < units % 3 else 0) for i in range(3)]
+    sizes = [units // count + (1 if i < units % count else 0) for i in range(count)]
     out, at = [], 0
     for size in sizes:
         if size:
@@ -34,7 +35,7 @@
 
 
 class AllReduce:
-    def __init__(self, src, recv, dst, sems, n_row, me, col):
+    def __init__(self, src, recv, dst, sems, n_row, me, col, count):
         self.src, self.recv, self.dst = src, recv, dst
         self.sems = sems
         self.n = n_row
@@ -43,7 +44,7 @@
         self.me = me
         self.chunks = []
         spin = max(self.bits - 1, 1)
-        for c, (ro, rn) in enumerate(row_chunks(src.shape[1])):
+        for c, (ro, rn) in enumerate(row_chunks(src.shape[1], count)):
             order = [(c + t) % spin for t in range(spin)] + list(range(spin, self.bits))
             starts = [0]
             mine = []
@@ -75,11 +76,11 @@
         for chunk in self.chunks:
             self.rs_copy(s, chunk).start()
 
-    def rs_finish(self, s):
+    def rs_finish(self, s, chunks):
         half = self.n >> (s + 1)
         off = self.n - (self.n >> s)
         last = s == self.bits - 1
-        for chunk in self.chunks:
+        for chunk in chunks:
             c, ro, rn, order, starts, mine = chunk
             self.rs_copy(s, chunk).wait()
             keep = starts[s + 1]
@@ -110,56 +111,122 @@
             device_id_type=MESH,
         )
 
-    def ag_finish(self, s):
-        for chunk in self.chunks:
+    def ag_finish(self, s, chunks):
+        for chunk in chunks:
             self.ag_copy(s, chunk).wait()
             if s > 0:
                 self.ag_copy(s - 1, chunk).start()
 
     def steps(self):
-        out = [functools.partial(self.rs_finish, s) for s in range(self.bits)]
-        out += [functools.partial(self.ag_finish, s) for s in reversed(range(self.bits))]
+        groups = [self.chunks[i : i + 3] for i in range(0, len(self.chunks), 3)]
+        out = []
+        for s in range(self.bits):
+            out += [functools.partial(self.rs_finish, s, group) for group in groups]
+        for s in reversed(range(self.bits)):
+            out += [functools.partial(self.ag_finish, s, group) for group in groups]
         return out
 
 
-def factor_panels(t_ref, k, lo, hi):
+def split3(x):
+    hi = x.astype(jnp.bfloat16).astype(jnp.float32)
+    rest = x - hi
+    mid = rest.astype(jnp.bfloat16).astype(jnp.float32)
+    return hi, mid, rest - mid
+
+
+def split2(x):
+    hi = x.astype(jnp.bfloat16)
+    return hi, (x - hi.astype(jnp.float32)).astype(jnp.bfloat16)
+
+
+def dot3(a, b):
+    def one(u, v):
+        return jnp.dot(u, v, preferred_element_type=jnp.float32)
+
+    return one(a[0], b[0]) + (one(a[0], b[1]) + one(a[1], b[0]))
+
+
+def eliminate(x, lane, sub):
+    d11 = d12 = d22 = None
+    for a in range(0, SUB, 2):
+        b = a + 1
+        ca = jnp.broadcast_to(x[:, a : a + 1], x.shape)
+        cb = jnp.broadcast_to(x[:, b : b + 1], x.shape)
+        p11 = jnp.broadcast_to(ca[a : a + 1, :], x.shape)
+        p12 = jnp.broadcast_to(cb[a : a + 1, :], x.shape)
+        p22 = jnp.broadcast_to(cb[b : b + 1, :], x.shape)
+        if a == 0:
+            d11, d12, d22 = p11, p12, p22
+        else:
+            here = sub >= a
+            d11 = jnp.where(here, p11, d11)
+            d12 = jnp.where(here, p12, d12)
+            d22 = jnp.where(here, p22, d22)
+        if b == SUB - 1:
+            break
+        below = sub > b
+        pair = (lane == a) | (lane == b)
+        row_a = jnp.where(pair, jnp.where(lane == a, 1.0, 0.0), jnp.broadcast_to(x[a : a + 1, :], x.shape))
+        row_b = jnp.where(pair, jnp.where(lane == b, 1.0, 0.0), jnp.broadcast_to(x[b : b + 1, :], x.shape))
+        r = jnp.where(below, 1.0 / (p11 * p22 - p12 * p12), 0.0)
+        num = (ca * p22 - cb * p12) * row_a + (cb * p11 - ca * p12) * row_b
+        x = jnp.where(pair & below, 0.0, x) - num * r
+    m = jnp.where(sub % 2 == 1, d12 / d11, 0.0)
+    scale = lax.rsqrt(jnp.where(sub % 2 == 1, d22 - d12 * m, d11))
+    y = jnp.where(lane == sub, 1.0, jnp.where(lane < sub - sub % 2, x, 0.0))
+    return (y - m * pltpu.roll(y, 1, 0)) * scale
+
+
+def factor_panels(t_ref, d_ref, k, lo, hi):
     base = k * LANE
+    end = base + LANE
     size = t_ref.shape[0]
     lane = lax.broadcasted_iota(jnp.int32, (SUB, LANE), 1)
     sub = lax.broadcasted_iota(jnp.int32, (SUB, LANE), 0)
-    wide_lane = lax.broadcasted_iota(jnp.int32, (SUB, size), 1)
-    wide_sub = lax.broadcasted_iota(jnp.int32, (SUB, size), 0)
+    full_lane = lax.broadcasted_iota(jnp.int32, (LANE, LANE), 1)
+    full_sub = lax.broadcasted_iota(jnp.int32, (LANE, LANE), 0)
+    if lo == 0:
+        d_ref[...] = t_ref[base:end, base:end]
 
     def one(p, carry):
-        r0 = pl.multiple_of(base + p * SUB, SUB)
-        pan = t_ref[pl.ds(r0, SUB), :]
-        x = pltpu.roll(pan[:, base : base + LANE], (LANE - p * SUB) % LANE, 1)
-        for j in range(SUB - 1):
-            col = x[:, j : j + 1]
-            m = jnp.where(sub[:, :1] > j, col / col[j : j + 1, :], 0.0)
-            row = jnp.where(lane[:1] == j, 1.0, x[j : j + 1, :])
-            x = jnp.where((lane == j) & (sub > j), 0.0, x) - m * row
-        diag = jnp.sum(jnp.where(lane == sub, x, 0.0), axis=1, keepdims=True)
-        scale = 1.0 / jnp.sqrt(diag)
-        inv = jnp.where(lane == sub, 1.0, jnp.where(lane < sub, x, 0.0)) * scale
-        rel = wide_lane - r0
+        r0 = pl.multiple_of(p * SUB, SUB)
+        pan = d_ref[pl.ds(r0, SUB), :]
+        inv = eliminate(pltpu.roll(pan, (LANE - r0) % LANE, 1), lane, sub)
+        rel = lane - r0
         inside = (rel >= 0) & (rel < SUB)
-        pan = jnp.where(inside, jnp.where(rel == wide_sub, 1.0, 0.0), pan)
-        top = inv[:, 0:1] * pan[0:1, :]
-        for j in range(1, SUB):
-            top = top + inv[:, j : j + 1] * pan[j : j + 1, :]
-        w = jnp.where(rel >= SUB, top, 0.0)
-        upd = dot(w[:, base:], top, 0, 0)
-        rel_all = lax.broadcasted_iota(jnp.int32, (size - base, size), 1) - r0
-        clear = (rel_all >= 0) & (rel_all < SUB)
-        t_ref[base:, :] = jnp.where(clear, 0.0, t_ref[base:, :]) - upd
-        t_ref[pl.ds(r0, SUB), :] = top
+        pan = jnp.where(inside, jnp.where(rel == sub, 1.0, 0.0), pan)
+        terms = [inv[:, j : j + 1] * pan[j : j + 1, :] for j in range(SUB)]
+        while len(terms) > 1:
+            terms = [terms[i] + terms[i + 1] for i in range(0, len(terms), 2)]
+        top = terms[0]
+        m1, m2, m3 = split3(top)
+        after = rel >= SUB
+        w1, w2, w3 = (jnp.where(after, v, 0.0) for v in (m1, m2, m3))
+        left = jnp.concatenate([w1, w1, w2, w1, w2, w3], axis=0).astype(jnp.bfloat16)
+        right = jnp.concatenate([m1, m2, m1, m3, m2, m1], axis=0).astype(jnp.bfloat16)
+        upd = lax.dot_general(
+            left, right, (((0,), (0,)), ((), ())), preferred_element_type=jnp.float32
+        )
+        clear = (full_lane >= r0) & (full_lane < r0 + SUB)
+        d_ref[...] = jnp.where(clear, 0.0, d_ref[...]) - upd
+        d_ref[pl.ds(r0, SUB), :] = top
         return carry
 
     lax.fori_loop(lo, hi, one, 0)
-
-
-def kernel(n_row, n_col, scale, a_ref, top_ref, basis_ref, a12, a12t, p, p_in, q, g, g_in, gq, t,
+    if hi * SUB == LANE:
+        inv = jnp.where(full_lane <= full_sub, d_ref[...], 0.0)
+        for c in range(size // LANE):
+            at = slice(c * LANE, (c + 1) * LANE)
+            if c != k:
+                t_ref[base:end, at] = dot(inv, t_ref[base:end, at])
+        t_ref[base:end, base:end] = inv
+        if end < size:
+            t_ref[end:, base:end] = jnp.zeros((size - end, LANE), jnp.float32)
+            low = t_ref[base:end, end:].T
+            t_ref[end:, :] = t_ref[end:, :] - dot(low, t_ref[base:end, :])
+
+
+def kernel(n_row, n_col, scale, a_ref, top_ref, basis_ref, a12, a12t, p, p_in, q, g, g_in, gq, t, d,
            p_sems, g_sems, bsend, brecv):
     me = lax.axis_index("row")
     col = lax.axis_index("col")
@@ -203,11 +270,13 @@
 
     a12t[...] = a12[...].T
 
-    def fill(dst, src, split):
+    def fill(dst, src, split, exact):
         pair = 2 * LANE
+        left = a12t[...] if exact else split2(a12t[...])
 
         def one(i, carry):
-            val = dot(a12t[...], src[:, pl.ds(pl.multiple_of(i * pair, pair), pair)])
+            cols = src[:, pl.ds(pl.multiple_of(i * pair, pair), pair)]
+            val = dot(left, cols) if exact else dot3(left, split2(cols))
             for h in range(2):
                 part = val[:, h * LANE : (h + 1) * LANE]
                 dst[pl.ds((2 * i + h) * split, split)] = part.reshape(split, WIDE // split, LANE)
@@ -215,39 +284,46 @@
 
         lax.fori_loop(0, src.shape[1] // pair, one, 0)
 
-    fill(g, a12, g_split)
-    g_red = AllReduce(g, g_in, gq, g_sems, n_row, me, col)
+    fill(g, a12, g_split, True)
+    g_red = AllReduce(g, g_in, gq, g_sems, n_row, me, col, 3)
     g_red.rs_start(0)
-    fill(p, a_ref, p_split)
+    fill(p, a_ref, p_split, False)
     for step in g_red.steps():
         step()
-    p_red = AllReduce(p, p_in, q, p_sems, n_row, me, col)
+    p_red = AllReduce(p, p_in, q, p_sems, n_row, me, col, P_CHUNKS)
     p_red.rs_start(0)
     for b in range(gblocks):
         t[:, b * LANE : (b + 1) * LANE] = gq[b * g_split : (b + 1) * g_split].reshape(WIDE, LANE)
 
+    rows = lax.broadcasted_iota(jnp.int32, (WIDE, WIDE), 0)
+    cols = lax.broadcasted_iota(jnp.int32, (WIDE, WIDE), 1)
+    diag = jnp.where(cols == rows, t[...], 0.0)
+    norm = lax.rsqrt(jnp.sum(diag, axis=0, keepdims=True))
+    t[...] = t[...] * lax.rsqrt(jnp.sum(diag, axis=1, keepdims=True)) * norm
+
     per = LANE // SUB
-    units = [(k, lo, lo + per // 2) for k in range(gblocks) for lo in (0, per // 2)]
+    few = per // 4
+    units = [(k, lo, lo + few) for k in range(gblocks) for lo in range(0, per, few)]
     steps = p_red.steps()
     done = 0
     for i, step in enumerate(steps):
         upto = len(units) * (i + 1) // len(steps)
         for unit in units[done:upto]:
-            factor_panels(t, *unit)
+            factor_panels(t, d, *unit)
         done = upto
         step()
 
-    rows = lax.broadcasted_iota(jnp.int32, (WIDE, WIDE), 0)
-    cols = lax.broadcasted_iota(jnp.int32, (WIDE, WIDE), 1)
-    t[...] = jnp.where(cols <= rows, t[...], 0.0)
+    t[...] = jnp.where(cols <= rows, t[...] * norm, 0.0)
     basis_ref[...] = dot(a12[...], t[...], 1, 1) * scale
+
+    inverse = split2(t[...])
 
     def finish(i, carry):
         pair = 2 * LANE
         parts = [
             q[pl.ds((2 * i + h) * p_split, p_split)].reshape(WIDE, LANE) for h in range(2)
         ]
-        val = dot(t[...], jnp.concatenate(parts, axis=1))
+        val = dot3(inverse, split2(jnp.concatenate(parts, axis=1)))
         r = lax.broadcasted_iota(jnp.int32, (WIDE, pair), 0)
         c = lax.broadcasted_iota(jnp.int32, (WIDE, pair), 1) + col * a_ref.shape[1] + i * pair
         top_ref[:, pl.ds(pl.multiple_of(i * pair, pair), pair)] = jnp.where(c >= r, val, 0.0)
@@ -282,7 +358,8 @@
             pltpu.VMEM(g_shape, f32),
             pltpu.VMEM(g_shape, f32),
             pltpu.VMEM((WIDE, WIDE), f32),
-            pltpu.SemaphoreType.DMA((4, bits, 3)),
+            pltpu.VMEM((LANE, LANE), f32),
+            pltpu.SemaphoreType.DMA((4, bits, P_CHUNKS)),
             pltpu.SemaphoreType.DMA((4, bits, 3)),
             pltpu.SemaphoreType.DMA((n_col,)),
             pltpu.SemaphoreType.DMA((1,)),

time: 164 us -> 131 us (0.80)
  Pallas kernels: 158 us -> 125 us
    pallas_call x1, Pallas kernels: 158 us -> 125 us  [body(): pl.pallas_call(functools.partial(kernel, n_row, n_col, scale), out_shape=...]
where the time goes in v1:
time: 131 us
  Pallas kernels  125 us (95%)
  local copies, waits for them, and re-layouts  5.55 us (4%)
    pallas_call x1, Pallas kernels, body(): pl.pallas_call(functools.partial(kernel, n_row, n_col, scale), out_shape=...  125 us
    unnamed x4, local copies, waits for them, and re-layouts  5.55 us

profile of v1, /device:TPU:0, one launch (start us, length us, event | category | flops | bytes accessed | tf_op | source)
XLA Modules:
  0.0 131.1 jit_solution(12998910697615873893)
XLA Ops:
  0.6 124.9 %shard_map.30 = (f32[512,2048]{1,0:T(8,128)}, f32[256,512]{1,0:T(8,128)}) custom-call(f32[256,2048]{1,0:T(8,128)} %a_ref.1), custom_call_target="tpu_custom_call" | custom-call | tf_op jit(solution)/shard_map/pallas_call | solution.py:343
  125.5 0.0 copy-start
  125.5 4.8 %copy.5 = f32[512,2048]{1,0:T(8,128)} copy(f32[512,2048]{1,0:T(8,128)} %get-tuple-element.4) | data formatting | bytes 8388608
  130.3 0.0 copy-done
  130.3 0.8 copy.6
Async XLA Ops:
  125.5 4.8 %copy-start = (f32[256,512]{1,0:T(8,128)S(1)}, f32[256,512]{1,0:T(8,128)}, u32[]{:S(2)}) copy-start(f32[256,512]{1,0:T(8,128)} %get-tuple-element.5) | copy-start | bytes 1572868

commit v2 on v1

--- a/solution.py
+++ b/solution.py
@@ -35,7 +35,7 @@
 
 
 class AllReduce:
-    def __init__(self, src, recv, dst, sems, n_row, me, col, count):
+    def __init__(self, src, recv, dst, sems, n_row, me, col, count, base=0, height=None):
         self.src, self.recv, self.dst = src, recv, dst
         self.sems = sems
         self.n = n_row
@@ -44,7 +44,8 @@
         self.me = me
         self.chunks = []
         spin = max(self.bits - 1, 1)
-        for c, (ro, rn) in enumerate(row_chunks(src.shape[1], count)):
+        for c, (ro, rn) in enumerate(row_chunks(height or src.shape[1], count)):
+            ro = pl.multiple_of(base + ro, SUB) if height else ro
             order = [(c + t) % spin for t in range(spin)] + list(range(spin, self.bits))
             starts = [0]
             mine = []
@@ -227,7 +228,7 @@
 
 
 def kernel(n_row, n_col, scale, a_ref, top_ref, basis_ref, a12, a12t, p, p_in, q, g, g_in, gq, t, d,
-           p_sems, g_sems, bsend, brecv):
+           p_sems, g_sems, bsend, brecv, xsend, xrecv):
     me = lax.axis_index("row")
     col = lax.axis_index("col")
     bits = n_row.bit_length() - 1
@@ -285,13 +286,34 @@
         lax.fori_loop(0, src.shape[1] // pair, one, 0)
 
     fill(g, a12, g_split, True)
-    g_red = AllReduce(g, g_in, gq, g_sems, n_row, me, col, 3)
+    shared = (g.shape[1] // SUB) % n_col == 0 and n_col > 1
+    g_high = g.shape[1] // n_col if shared else None
+    g_base = col * g_high if shared else 0
+    g_red = AllReduce(g, g_in, gq, g_sems, n_row, me, col, 3, g_base, g_high)
     g_red.rs_start(0)
     fill(p, a_ref, p_split, False)
     for step in g_red.steps():
         step()
+    if shared:
+        part = gq.at[:, pl.ds(pl.multiple_of(g_base, SUB), g_high), :]
+        swaps = [
+            pltpu.make_async_remote_copy(
+                src_ref=part,
+                dst_ref=part,
+                send_sem=xsend.at[c],
+                recv_sem=xrecv.at[c],
+                device_id=(me, (col + c) % n_col),
+                device_id_type=MESH,
+            )
+            for c in range(1, n_col)
+        ]
+        for swap in swaps:
+            swap.start()
     p_red = AllReduce(p, p_in, q, p_sems, n_row, me, col, P_CHUNKS)
     p_red.rs_start(0)
+    if shared:
+        for swap in swaps:
+            swap.wait()
     for b in range(gblocks):
         t[:, b * LANE : (b + 1) * LANE] = gq[b * g_split : (b + 1) * g_split].reshape(WIDE, LANE)
 
@@ -363,6 +385,8 @@
             pltpu.SemaphoreType.DMA((4, bits, 3)),
             pltpu.SemaphoreType.DMA((n_col,)),
             pltpu.SemaphoreType.DMA((1,)),
+            pltpu.SemaphoreType.DMA((n_col,)),
+            pltpu.SemaphoreType.DMA((n_col,)),
         ],
         compiler_params=pltpu.CompilerParams(
             collective_id=0, has_side_effects=True, vmem_limit_bytes=60 * 1024 * 1024

time: 131 us -> 124 us (0.947)
  Pallas kernels: 125 us -> 118 us
    pallas_call x1, Pallas kernels: 125 us -> 118 us  [body(): pl.pallas_call(functools.partial(kernel, n_row, n_col, scale), out_shape=...]
where the time goes in v2:
time: 124 us
  Pallas kernels  118 us (95%)
  local copies, waits for them, and re-layouts  5.55 us (4%)
    pallas_call x1, Pallas kernels, body(): pl.pallas_call(functools.partial(kernel, n_row, n_col, scale), out_shape=...  118 us
    unnamed x4, local copies, waits for them, and re-layouts  5.55 us

profile of v2, /device:TPU:0, one launch (start us, length us, event | category | flops | bytes accessed | tf_op | source)
XLA Modules:
  0.0 124.1 jit_solution(13470583025764196333)
XLA Ops:
  0.6 117.9 %shard_map.30 = (f32[512,2048]{1,0:T(8,128)}, f32[256,512]{1,0:T(8,128)}) custom-call(f32[256,2048]{1,0:T(8,128)} %a_ref.1), custom_call_target="tpu_custom_call" | custom-call | tf_op jit(solution)/shard_map/pallas_call | solution.py:365
  118.5 0.0 copy-start
  118.5 4.8 %copy.5 = f32[512,2048]{1,0:T(8,128)} copy(f32[512,2048]{1,0:T(8,128)} %get-tuple-element.4) | data formatting | bytes 8388608
  123.3 0.0 copy-done
  123.3 0.8 copy.6
Async XLA Ops:
  118.5 4.8 %copy-start = (f32[256,512]{1,0:T(8,128)S(1)}, f32[256,512]{1,0:T(8,128)}, u32[]{:S(2)}) copy-start(f32[256,512]{1,0:T(8,128)} %get-tuple-element.5) | copy-start | bytes 1572868

commit v3 on v2

--- a/solution.py
+++ b/solution.py
@@ -329,14 +329,15 @@
     steps = p_red.steps()
     done = 0
     for i, step in enumerate(steps):
-        upto = len(units) * (i + 1) // len(steps)
+        upto = min(len(units) * (i + 1) // (len(steps) - 2), len(units))
         for unit in units[done:upto]:
             factor_panels(t, d, *unit)
         done = upto
+        if i == len(steps) - 2:
+            t[...] = jnp.where(cols <= rows, t[...] * norm, 0.0)
+            basis_ref[...] = dot(a12[...], t[...], 1, 1) * scale
         step()
 
-    t[...] = jnp.where(cols <= rows, t[...] * norm, 0.0)
-    basis_ref[...] = dot(a12[...], t[...], 1, 1) * scale
 
     inverse = split2(t[...])
 

time: 124 us -> 126 us (1.016)
  Pallas kernels: 118 us -> 120 us
    pallas_call x1, Pallas kernels: 118 us -> 120 us  [body(): pl.pallas_call(functools.partial(kernel, n_row, n_col, scale), out_shape=...]
where the time goes in v3:
time: 126 us
  Pallas kernels  120 us (95%)
  local copies, waits for them, and re-layouts  5.55 us (4%)
    pallas_call x1, Pallas kernels, body(): pl.pallas_call(functools.partial(kernel, n_row, n_col, scale), out_shape=...  120 us
    unnamed x4, local copies, waits for them, and re-layouts  5.55 us

profile of v3, /device:TPU:0, one launch (start us, length us, event | category | flops | bytes accessed | tf_op | source)
XLA Modules:
  0.0 125.8 jit_solution(16742401993228785451)
XLA Ops:
  0.6 119.6 %shard_map.30 = (f32[512,2048]{1,0:T(8,128)}, f32[256,512]{1,0:T(8,128)}) custom-call(f32[256,2048]{1,0:T(8,128)} %a_ref.1), custom_call_target="tpu_custom_call" | custom-call | tf_op jit(solution)/shard_map/pallas_call | solution.py:366
  120.3 0.0 copy-start
  120.3 4.8 %copy.5 = f32[512,2048]{1,0:T(8,128)} copy(f32[512,2048]{1,0:T(8,128)} %get-tuple-element.4) | data formatting | bytes 8388608
  125.1 0.0 copy-done
  125.1 0.8 copy.6
Async XLA Ops:
  120.3 4.8 %copy-start = (f32[256,512]{1,0:T(8,128)S(1)}, f32[256,512]{1,0:T(8,128)}, u32[]{:S(2)}) copy-start(f32[256,512]{1,0:T(8,128)} %get-tuple-element.5) | copy-start | bytes 1572868
